TPU v7x, 32 devices: a whole 2x2x4 slice. The times are simulated.
32 devices in a mesh: groups: 2 (over x), ctx: 16 (over z, y, core).
Axes of the slice: x: 2, y: 2, z: 4, core: 2. Of those that a mesh axis runs over, the one named last changes fastest.
Arguments:
- tokens: bfloat16 [3072, 1152], P(('groups', 'ctx')), parts along dimension 0, may hold values from -100 to 100
- owner: int32 [3072, 1], P(('groups', 'ctx')), parts along dimension 0, may hold values from 0 to 15; in each aligned block of 96 rows (0 to 95, 96 to 191, ...) at most 12 rows name the same one
- slot_map: int32 [32, 16, 12], P(('groups', 'ctx')), parts along dimension 0, may hold values from 0 to 47
- sizes: int32 [3072], P(('groups', 'ctx')), parts along dimension 0, may hold values from 1 to 4
- w_query: bfloat16 [1152, 576], replicated, may hold values from -0.1875 to 0.1875
- w_key: bfloat16 [1152, 576], replicated, may hold values from -0.1875 to 0.1875
- w_value: bfloat16 [1152, 576], replicated, may hold values from -0.1875 to 0.1875
- w_out: bfloat16 [576, 1152], replicated, may hold values from -0.25 to 0.25
Outputs:
- mixed: bfloat16 [3072, 1152], P(('groups', 'ctx')), parts along dimension 0
There are 2 independent parts, one for each index of `groups`. A program takes and returns all parts, laid end to end along the dimension named above; an argument that names none is the same for every part. Nothing has to cross between parts.
Inputs may be any that keep to these rules, and one draw needn't show every extreme that they name: Among the source tokens of one index of ctx, at most 12 name the same owner, and in some index exactly 12 do.
All inputs are finite; a program needn't handle non-finite values.
Results may differ from a plain program's by a relative error of at most 0.0085.
The roundings to bfloat16 on the way count: a program that leaves them out, or rounds other values in their place, can miss the bound.
Values may be sent and summed in bfloat16 or wider, within the bound.
A program may use at most 128 MiB of HBM per device.

v0:
```python
import math

import jax
import jax.numpy as jnp
from jax import lax
from jax.sharding import PartitionSpec as P

HEADS = 8
HEAD = 72


def on_device(tokens, owner, slot_map, sizes, w_query, w_key, w_value, w_out):
    tok_rows = tokens.shape[0]
    shards = lax.axis_size("ctx")
    slots = slot_map.shape[2]
    places = shards * slots
    merged_rows = tok_rows // 2
    owners = owner[:, 0]
    marks = (owners[:, None] == jnp.arange(shards, dtype=jnp.int32)[None, :]).astype(jnp.int32)
    ranking = jnp.sum((jnp.cumsum(marks, axis=0) - marks) * marks, axis=1)
    bucket = owners * slots + ranking
    to_bucket = (bucket[:, None] == jnp.arange(places, dtype=jnp.int32)[None, :]).astype(
        jnp.bfloat16
    )
    outgoing = jnp.einsum(
        "tp,td->pd", to_bucket, tokens, preferred_element_type=jnp.float32
    ).astype(jnp.bfloat16)
    out_weights = jnp.einsum(
        "tp,t->p", to_bucket, sizes.astype(jnp.bfloat16), preferred_element_type=jnp.float32
    ).astype(jnp.bfloat16)
    received, in_weights = (
        lax.all_to_all(
            outgoing.reshape(shards, slots, -1), "ctx", split_axis=0, concat_axis=0, tiled=True
        ),
        lax.all_to_all(
            out_weights.reshape(shards, slots), "ctx", split_axis=0, concat_axis=0, tiled=True
        ),
    )
    targets = slot_map[0].reshape(places)
    landing = targets[None, :] == jnp.arange(merged_rows, dtype=jnp.int32)[:, None]
    weighted = jnp.where(landing, in_weights.reshape(places)[None, :], 0)
    merged_sum = jnp.dot(weighted, received.reshape(places, -1), preferred_element_type=jnp.float32)
    counts = jnp.sum(weighted.astype(jnp.float32), axis=1)
    merged = (merged_sum / jnp.maximum(counts, 1.0)[:, None]).astype(jnp.bfloat16)
    key_bias = jnp.where(counts > 0, jnp.log(jnp.maximum(counts, 1.0)), -1e30).astype(jnp.bfloat16)
    queries = jnp.dot(merged, w_query, preferred_element_type=jnp.float32).astype(jnp.bfloat16)
    query_heads = queries.reshape(merged_rows, HEADS, HEAD)
    inverse = 1.0 / math.sqrt(HEAD)

    def attend_block(carry, item):
        row_max, total, accum = carry
        key_heads, value_heads, bias = item
        scores = (
            jnp.einsum("qhd,khd->hqk", query_heads, key_heads, preferred_element_type=jnp.float32)
            * inverse
        )
        scores = scores + bias.astype(jnp.float32)[None, None, :]
        new_max = jnp.maximum(row_max, jnp.max(scores, axis=2))
        factor = jnp.exp(row_max - new_max)
        expo = jnp.exp(scores - new_max[:, :, None])
        total = total * factor + jnp.sum(expo, axis=2)
        accum = accum * factor[:, :, None] + jnp.einsum(
            "hqk,khd->hqd",
            expo.astype(jnp.bfloat16),
            value_heads,
            preferred_element_type=jnp.float32,
        )
        return ((new_max, total, accum), None)

    start_state = (
        jnp.full((HEADS, merged_rows), -jnp.inf, jnp.float32),
        jnp.zeros((HEADS, merged_rows), jnp.float32),
        jnp.zeros((HEADS, merged_rows, HEAD), jnp.float32),
    )
    own_keys = jnp.dot(merged, w_key, preferred_element_type=jnp.float32).astype(jnp.bfloat16)
    own_values = jnp.dot(merged, w_value, preferred_element_type=jnp.float32).astype(jnp.bfloat16)
    carry = start_state
    keys = lax.all_gather(own_keys, "ctx", axis=0, tiled=True)
    values = lax.all_gather(own_values, "ctx", axis=0, tiled=True)
    bias = lax.all_gather(key_bias, "ctx", axis=0, tiled=True)
    length = keys.shape[0]
    block = math.gcd(length, 1536)
    turns = length // block
    items = (
        keys.reshape(turns, block, HEADS, HEAD),
        values.reshape(turns, block, HEADS, HEAD),
        bias.reshape(turns, block),
    )
    carry, unused = lax.scan(attend_block, carry, items)
    row_max, total, accum = carry
    attended = (
        jnp.transpose(accum / total[:, :, None], (1, 0, 2))
        .reshape(merged_rows, HEADS * HEAD)
        .astype(jnp.bfloat16)
    )
    landing_rows = landing.astype(jnp.bfloat16)
    leaving = jnp.einsum(
        "mp,md->pd", landing_rows, attended, preferred_element_type=jnp.float32
    ).astype(jnp.bfloat16)
    returned = lax.all_to_all(
        leaving.reshape(shards, slots, -1), "ctx", split_axis=0, concat_axis=0, tiled=True
    )
    picked = jnp.einsum(
        "tp,pd->td", to_bucket, returned.reshape(places, -1), preferred_element_type=jnp.float32
    ).astype(jnp.bfloat16)
    mixed = jnp.dot(picked, w_out, preferred_element_type=jnp.float32).astype(jnp.bfloat16)
    return mixed


def solution(mesh):
    in_specs = (
        P(("groups", "ctx"), None),
        P(("groups", "ctx"), None),
        P(("groups", "ctx"), None, None),
        P(("groups", "ctx")),
        P(),
        P(),
        P(),
        P(),
    )
    out_specs = P(("groups", "ctx"), None)
    return jax.shard_map(
        on_device, mesh=mesh, in_specs=in_specs, out_specs=out_specs, check_vma=False
    )
```

profile of v0, /device:TPU:0, one launch (start us, length us, event | category | flops | bytes accessed | tf_op | source)
XLA Modules:
  0.0 126.5 jit_solution(1130961317788527914)
XLA Ops:
  0.0 0.8 fusion.16
  1.0 0.8 select_reduce_fusion
  1.8 0.7 fusion.23
  2.5 0.8 fusion.10
  3.3 0.7 all_to_all.16
  4.1 7.4 %all-to-all-start = ((bf16[16,1,12]{2,1,0:T(2,128)(2,1)}), bf16[16,1,12]{2,1,0:T(2,128)(2,1)S(1)}, u32[]{:S(2)}, u32[]{:S(2)}) async-start(bf16[16,1,12]{2,1,0:T(2,128)(2,1)} %all_to_all.16), calls=%async_computation | async-start | bytes 16384 | tf_op jit(solution)/shard_map/all_to_all | solution.py:35
  11.5 1.3 %convolution_convert_fusion = bf16[192,1152]{1,0:T(8,128)(2,1)S(1)} fusion(bf16[96,1152]{1,0:T(8,128)(2,1)} %param.8, s32[96]{0:T(128)S(1)} %fusion.23), kind=kOutput, calls=%fused_computation | convolution fusion | flops 42706944 | bytes 663936 | tf_op jit(solution)/shard_map/tp,td->pd/dot_general | solution.py:25
  12.8 0.9 reshape.49
  13.8 4.1 %all-to-all-done = bf16[16,1,12]{2,1,0:T(2,128)(2,1)S(1)} async-done(((bf16[16,1,12]{2,1,0:T(2,128)(2,1)}), bf16[16,1,12]{2,1,0:T(2,128)(2,1)S(1)}, u32[]{:S(2)}, u32[]{:S(2)}) %all-to-all-start) | async-done | bytes 416 | tf_op jit(solution)/shard_map/all_to_all | solution.py:35
  17.8 3.6 %all-to-all-start.1 = ((bf16[16,12,1152]{2,1,0:T(8,128)(2,1)}), bf16[16,12,1152]{2,1,0:T(8,128)(2,1)S(1)}, u32[]{:S(2)}, u32[]{:S(2)}) async-start(bf16[16,12,1152]{2,1,0:T(8,128)(2,1)} %reshape.49), calls=%async_computation.1 | async-start | bytes 1179648 | tf_op jit(solution)/shard_map/all_to_all | solution.py:32
  21.6 0.6 dynamic-slice.1
  23.4 35.8 %all-reduce = bf16[768]{0:T(1024)(128)(2,1)S(1)} all-reduce(bf16[768]{0:T(1024)(128)(2,1)S(1)} %dynamic-update-slice), channel_id=1, replica_groups=mesh['groups'=2,'ctx'=16] {'ctx'}, use_global_device_ids=true, to_apply=%add | all-reduce | flops 768 | bytes 3072
  59.2 0.9 reshape.50
  60.1 1.2 fusion
  61.3 0.5 convolution_convert_fusion.4
  61.8 20.4 %all_gather.11 = bf16[768,576]{1,0:T(8,128)(2,1)S(1)} all-gather(bf16[48,576]{1,0:T(8,128)(2,1)S(1)} %convolution_convert_fusion.4), channel_id=1, replica_groups=mesh['groups'=2,'ctx'=16] {'ctx'}, dimensions={0}, use_global_device_ids=true | all-gather | bytes 940032 | tf_op jit(solution)/shard_map/all_gather | solution.py:79
  82.2 1.3 %copy.27 = bf16[768,576]{0,1:T(8,128)(2,1)} copy(bf16[768,576]{1,0:T(8,128)(2,1)S(1)} %all_gather.11) | data formatting | bytes 1769472 | tf_op jit(solution)/shard_map/all_gather | solution.py:79
  83.4 1.8 %convolution_convert_fusion.5 = bf16[48,576]{1,0:T(8,128)(2,1)S(1)} fusion(bf16[48,1152]{1,0:T(8,128)(2,1)S(1)} %fusion, bf16[1152,576]{0,1:T(8,128)(2,1)} %param.13), kind=kOutput, calls=%fused_computation.14 | convolution fusion | flops 63728640 | bytes 1492992 | tf_op jit(solution)/shard_map/dot_general | solution.py:75
  85.2 21.5 %all_gather.9 = bf16[768,576]{1,0:T(8,128)(2,1)S(1)} all-gather(bf16[48,576]{1,0:T(8,128)(2,1)S(1)} %convolution_convert_fusion.5), channel_id=1, replica_groups=mesh['groups'=2,'ctx'=16] {'ctx'}, dimensions={0}, use_global_device_ids=true | all-gather | bytes 940032 | tf_op jit(solution)/shard_map/all_gather | solution.py:78
  106.8 0.6 copy.25
  107.4 1.8 %convolution_convert_fusion.6 = bf16[48,576]{1,0:T(8,128)(2,1)S(1)} fusion(bf16[48,1152]{1,0:T(8,128)(2,1)S(1)} %fusion, bf16[1152,576]{0,1:T(8,128)(2,1)} %param.12), kind=kOutput, calls=%fused_computation.15 | convolution fusion | flops 63728640 | bytes 1492992 | tf_op jit(solution)/shard_map/dot_general | solution.py:46
  110.5 0.4 fusion.4
  111.4 13.7 %all_to_all.20 = bf16[16,12,576]{2,1,0:T(8,128)(2,1)S(1)} all-to-all(bf16[16,12,576]{2,1,0:T(8,128)(2,1)S(1)} %reshape.52), channel_id=1, replica_groups=mesh['groups'=2,'ctx'=16] {'ctx'}, dimensions={0} | all-to-all | bytes 442368 | tf_op jit(solution)/shard_map/all_to_all | solution.py:100
  125.2 1.2 convolution_convert_fusion.1
  (32 shorter events, 2.7 us)
Async XLA Ops:
  0.0 125.2 %copy-start = (bf16[576,1152]{1,0:T(8,128)(2,1)S(1)}, bf16[576,1152]{1,0:T(8,128)(2,1)}, u32[]{:S(2)}) copy-start(bf16[576,1152]{1,0:T(8,128)(2,1)} %param.15) | copy-start | bytes 3981316
  4.1 13.8 %all-to-all-start = ((bf16[16,1,12]{2,1,0:T(2,128)(2,1)}), bf16[16,1,12]{2,1,0:T(2,128)(2,1)S(1)}, u32[]{:S(2)}, u32[]{:S(2)}) async-start(bf16[16,1,12]{2,1,0:T(2,128)(2,1)} %all_to_all.16), calls=%async_computation | async-start | bytes 16384 | tf_op jit(solution)/shard_map/all_to_all | solution.py:35
  11.5 10.0 %copy-start.3 = (s32[1,16,12]{1,0,2:T(1,128)S(1)}, s32[1,16,12]{1,0,2:T(1,128)}, u32[]{:S(2)}) copy-start(s32[1,16,12]{1,0,2:T(1,128)} %param.10) | copy-start | bytes 2308
  11.5 10.1 %copy-start.4 = (u32[32]{0:T(128)S(1)}, u32[32]{0:T(128)}, u32[]{:S(2)}) copy-start(u32[32]{0:T(128)} %constant.40) | copy-start | bytes 388
  17.8 41.4 %all-to-all-start.1 = ((bf16[16,12,1152]{2,1,0:T(8,128)(2,1)}), bf16[16,12,1152]{2,1,0:T(8,128)(2,1)S(1)}, u32[]{:S(2)}, u32[]{:S(2)}) async-start(bf16[16,12,1152]{2,1,0:T(8,128)(2,1)} %reshape.49), calls=%async_computation.1 | async-start | bytes 1179648 | tf_op jit(solution)/shard_map/all_to_all | solution.py:32
  21.4 39.9 %copy-start.1 = (bf16[1152,576]{0,1:T(8,128)(2,1)S(1)}, bf16[1152,576]{0,1:T(8,128)(2,1)}, u32[]{:S(2)}) copy-start(bf16[1152,576]{0,1:T(8,128)(2,1)} %param.14) | copy-start | bytes 3981316
  109.3 1.2 copy-start.2
where the time goes:
time: 127 us; the launch traced here: 126 us
  blocking collectives  91.4 us (72%)
  starting transfers between devices  11 us (9%)
  matrix products  9.81 us (8%)
  local copies, waits for them, and re-layouts  6.33 us (5%)
  waiting for transfers between devices  4.09 us (3%)
  other arithmetic  3.01 us (2%)
    unnamed x1, blocking collectives  35.8 us
    all_gather x1, blocking collectives, on_device(): keys = lax.all_gather(own_keys, 'ctx', axis=0, tiled=True)  21.5 us
    all_gather x1, blocking collectives, on_device(): values = lax.all_gather(own_values, 'ctx', axis=0, tiled=True)  20.4 us
    all_to_all x1, blocking collectives, on_device(): lax.all_to_all(leaving.reshape(shards, slots, -1), 'ctx', split_axis=0, c...  13.7 us
    all_to_all x1, starting transfers between devices, on_device(): lax.all_to_all(out_weights.reshape(shards, slots), 'ctx', split_axis=0, c...  7.41 us
    all_to_all x1, waiting for transfers between devices, on_device(): lax.all_to_all(out_weights.reshape(shards, slots), 'ctx', split_axis=0, c...  4.09 us
    all_to_all x1, starting transfers between devices, on_device(): lax.all_to_all(outgoing.reshape(shards, slots, -1), 'ctx', split_axis=0,...  3.58 us
  transfers between devices with their start and end apart: 2, of which 1 were waited for; matrix products, arithmetic and copies ran while one was open for 3% of the time, Pallas kernels for 0%

commit v1 on v0

v1 whole, which is shorter than its diff:
```python
import functools
import math

import jax
import jax.numpy as jnp
from jax import lax
from jax.experimental import pallas as pl
from jax.experimental.pallas import tpu as pltpu
from jax.sharding import PartitionSpec as P

HEADS = 8
HEAD = 72
LANES = 128
MESH = pl.DeviceIdType.MESH


def iota(shape, axis):
    return lax.broadcasted_iota(jnp.int32, shape, axis)


def kernel(
    shards,
    tok_ref,
    owner_ref,
    slot_ref,
    sizes_ref,
    wq_hbm,
    wk_hbm,
    wv_hbm,
    wo_hbm,
    out_ref,
    wq,
    wk,
    wv,
    wo,
    wo_pad,
    slots_in,
    outgoing,
    incoming,
    landed,
    dest_out,
    dest_in,
    heads_out,
    heads_in,
    att_out,
    att_in,
    w_sem,
    slot_send,
    slot_recv,
    tok_send,
    tok_recv,
    dest_send,
    dest_recv,
    head_send,
    head_recv,
    share_send,
    att_send,
    att_recv,
    own_sem,
):
    group = lax.axis_index("groups")
    me = lax.axis_index("ctx")
    reps = shards // HEADS
    my_head = me // reps
    my_rep = lax.rem(me, reps)
    tokens, width = tok_ref.shape
    slots = slot_ref.shape[2]
    padded = landed.shape[0] // shards
    places = landed.shape[0]
    merged_rows = heads_out.shape[1]
    total_rows = shards * merged_rows
    model = HEADS * HEAD
    pack = heads_out.shape[2]

    def remote(src, dst, send, recv, target):
        return pltpu.make_async_remote_copy(
            src_ref=src,
            dst_ref=dst,
            send_sem=send,
            recv_sem=recv,
            device_id=(group, target),
            device_id_type=MESH,
        )

    weights = [
        pltpu.make_async_copy(src, dst, w_sem.at[i])
        for i, (src, dst) in enumerate(
            ((wq_hbm, wq), (wk_hbm, wk), (wv_hbm, wv), (wo_hbm, wo))
        )
    ]
    for copy in weights:
        copy.start()

    barrier = pltpu.get_barrier_semaphore()

    @pl.loop(1, shards)
    def _(step):
        peer = lax.rem(me + step, shards)
        pl.semaphore_signal(barrier, inc=1, device_id=(group, peer), device_id_type=MESH)

    own_col = owner_ref[...]
    diag = iota((tokens, tokens), 0) == iota((tokens, tokens), 1)
    before = iota((tokens, tokens), 0) < iota((tokens, tokens), 1)
    own_row = jnp.sum(jnp.where(diag, own_col, 0), axis=0, keepdims=True)
    same = jnp.logical_and(own_col == own_row, before)
    rank_row = jnp.sum(jnp.where(same, 1, 0), axis=0, keepdims=True)
    place_row = own_row * padded + rank_row
    chosen = iota((places, tokens), 0) == place_row
    size_row = sizes_ref[...].astype(jnp.float32)
    size_col = jnp.sum(jnp.where(chosen, size_row, 0.0), axis=1, keepdims=True)
    size_tile = jnp.where(iota((places, LANES), 1) == 0, size_col, 0.0).astype(jnp.bfloat16)
    bucketed = jnp.dot(
        chosen.astype(jnp.float32).astype(jnp.bfloat16),
        tok_ref[...],
        preferred_element_type=jnp.float32,
    ).astype(jnp.bfloat16)
    for o in range(shards):
        rows = slice(o * padded, o * padded + slots)
        outgoing[o, :, 0:width] = bucketed[rows]
        outgoing[o, :, width : width + LANES] = size_tile[rows]

    pl.semaphore_wait(barrier, shards - 1)

    @pl.loop(1, shards)
    def _(step):
        peer = lax.rem(me + step, shards)
        remote(
            slot_ref.at[0], slots_in.at[me], slot_send.at[peer], slot_recv.at[me], peer
        ).start()
        remote(
            outgoing.at[peer], incoming.at[me], tok_send.at[peer], tok_recv.at[me], peer
        ).start()

    slots_in[me] = slot_ref[0]
    incoming[me] = outgoing[me]
    landed[...] = jnp.zeros_like(landed)
    wo_pad[...] = jnp.zeros_like(wo_pad)
    weights[3].wait()
    lead = 3 * HEAD - HEAD - LANES
    for h in range(HEADS):
        wo_pad[h, lead : lead + HEAD, :] = wo[h]

    @pl.loop(1, shards)
    def _(step):
        peer = lax.rem(me + step, shards)
        remote(
            slot_ref.at[0], slots_in.at[peer], slot_send.at[peer], slot_recv.at[peer], peer
        ).wait()

    tables = slots_in[...]
    table = jnp.sum(jnp.where(iota(tables.shape, 1) == me, tables, 0), axis=1)
    found = jnp.zeros((shards, tokens), jnp.int32)
    for r in range(slots):
        found = found + jnp.where(rank_row == r, table[:, r : r + 1], 0)
    found = jnp.where(iota((shards, tokens), 0) == own_row, found, 0)
    dest_row = own_row * merged_rows + jnp.sum(found, axis=0, keepdims=True)
    dest_out[:, 0:tokens] = jnp.broadcast_to(dest_row, (dest_out.shape[0], tokens))
    if tokens < dest_out.shape[1]:
        rest = dest_out.shape[1] - tokens
        dest_out[:, tokens:] = jnp.zeros((dest_out.shape[0], rest), jnp.int32)

    @pl.loop(1, HEADS)
    def _(step):
        head = lax.rem(my_head + step, HEADS)
        remote(
            dest_out, dest_in.at[my_head], dest_send.at[head], dest_recv.at[my_head],
            head * reps + my_rep,
        ).start()

    dest_in[my_head] = dest_out[...]

    own_table = slot_ref[0]
    lane = iota((shards, places), 1)
    target = jnp.zeros((shards, places), jnp.int32)
    for r in range(slots):
        target = target + jnp.where(lax.rem(lane, padded) == r, own_table[:, r : r + 1], 0)
    target = jnp.where(lane // padded == iota((shards, places), 0), target, 0)
    target_row = jnp.sum(target, axis=0, keepdims=True)
    landing = iota((merged_rows, places), 0) == target_row

    @pl.loop(1, shards)
    def _(step):
        peer = lax.rem(me + shards - step, shards)
        remote(
            outgoing.at[peer], incoming.at[peer], tok_send.at[peer], tok_recv.at[peer], peer
        ).wait()

    for e in range(shards):
        landed[e * padded : e * padded + slots, :] = incoming[e]
    pick = jnp.where(iota((8, LANES), 1) == 0, 1.0, 0.0).astype(jnp.bfloat16)
    weight_row = lax.dot_general(
        pick,
        landed[:, width : width + LANES],
        (((1,), (1,)), ((), ())),
        preferred_element_type=jnp.float32,
    )[0:1]
    weighted = jnp.where(landing, weight_row, 0.0)
    counts = jnp.sum(weighted, axis=1, keepdims=True)
    merged_sum = jnp.dot(
        weighted.astype(jnp.bfloat16), landed[:, 0:width], preferred_element_type=jnp.float32
    )
    merged = (merged_sum / jnp.maximum(counts, 1.0)).astype(jnp.bfloat16)
    bias = jnp.where(counts > 0, jnp.log(jnp.maximum(counts, 1.0)), -1e30)
    for copy in weights[:3]:
        copy.wait()
    spare = -model % LANES
    zeros = jnp.zeros((merged_rows, spare), jnp.float32)
    projected = [
        jnp.concatenate(
            [jnp.dot(merged, w[...], preferred_element_type=jnp.float32), zeros], axis=1
        )
        for w in (wq, wk, wv)
    ]
    lane = iota((merged_rows, pack), 1)
    for h in range(HEADS):
        block = jnp.where(lane == 3 * HEAD, bias, 0.0)
        first = h * HEAD // LANES * LANES
        for part in (2, 1, 0):
            window = projected[part][:, first : first + pack]
            shift = (part * HEAD - (h * HEAD - first)) % pack
            turned = pltpu.roll(window, shift, 1) if shift else window
            inside = jnp.logical_and(lane >= part * HEAD, lane < (part + 1) * HEAD)
            block = jnp.where(inside, turned, block)
        heads_out[h] = block.astype(jnp.bfloat16)

    @pl.loop(1, HEADS)
    def _(step):
        head = lax.rem(my_head + step, HEADS)
        remote(
            heads_out.at[head], heads_in.at[me], head_send.at[head], head_recv.at[me],
            head * reps + my_rep,
        ).start()

    heads_in[me] = heads_out[my_head]

    def share(step, source):
        partner = my_head * reps + lax.rem(my_rep + step, reps)
        return remote(
            heads_in.at[source],
            heads_in.at[source],
            share_send.at[step * shards + source],
            head_recv.at[source],
            partner,
        )

    @pl.loop(1, reps)
    def _(step):
        partner = my_head * reps + lax.rem(my_rep + step, reps)
        remote(
            heads_out.at[my_head],
            heads_in.at[me],
            share_send.at[step * shards + me],
            head_recv.at[me],
            partner,
        ).start()

    @pl.loop(1, HEADS)
    def _(step):
        source = lax.rem(my_head + HEADS - step, HEADS) * reps + my_rep
        remote(
            heads_out.at[my_head], heads_in.at[source], head_send.at[my_head],
            head_recv.at[source], source,
        ).wait_recv()

        @pl.loop(1, reps)
        def _(turn):
            share(turn, source).start()

    @pl.loop(1, HEADS)
    def _(step):
        other = lax.rem(my_head + HEADS - step, HEADS)
        remote(
            dest_out, dest_in.at[other], dest_send.at[other], dest_recv.at[other],
            other * reps + my_rep,
        ).wait()

    @pl.loop(1, reps)
    def _(step):
        rep = lax.rem(my_rep + reps - step, reps)

        @pl.loop(0, HEADS)
        def _(turn):
            source = lax.rem(my_head + HEADS - turn, HEADS) * reps + rep
            remote(
                heads_out.at[my_head], heads_in.at[source], head_send.at[my_head],
                head_recv.at[source], my_head * reps + rep,
            ).wait_recv()

    every = heads_in[...].reshape(total_rows, pack)
    pick = jnp.where(iota((8, pack), 1) == 3 * HEAD, 1.0, 0.0).astype(jnp.bfloat16)
    bias_row = lax.dot_general(
        pick, every, (((1,), (1,)), ((), ())), preferred_element_type=jnp.float32
    )[0:1]
    inverse = 1.0 / math.sqrt(HEAD)
    batch = HEADS // 2

    for turn in range(2):
        cols = []
        for b in range(batch):
            j = lax.rem(my_head + 1 + turn * batch + b, HEADS)
            row = dest_in[j][0:1, 0:tokens]
            cols.append(jnp.sum(jnp.where(diag, row, 0), axis=1, keepdims=True))
        column = jnp.concatenate(cols, axis=0)
        chosen = iota((batch * tokens, total_rows), 1) == column
        asked = jnp.dot(
            chosen.astype(jnp.float32).astype(jnp.bfloat16),
            every,
            preferred_element_type=jnp.float32,
        )
        asked = pltpu.roll(asked, HEAD, 1)
        lane = iota(asked.shape, 1)
        inside = jnp.logical_and(lane >= HEAD, lane < 2 * HEAD)
        asked = jnp.where(inside, asked, 0.0).astype(jnp.bfloat16)
        scores = lax.dot_general(
            asked, every, (((1,), (1,)), ((), ())), preferred_element_type=jnp.float32
        )
        scores = scores * inverse + bias_row
        expo = jnp.exp(scores - jnp.max(scores, axis=1, keepdims=True))
        total = jnp.sum(expo, axis=1, keepdims=True)
        accum = jnp.dot(
            expo.astype(jnp.bfloat16), every[:, LANES:], preferred_element_type=jnp.float32
        )
        attended = (accum / total).astype(jnp.bfloat16)
        for b in range(batch):
            j = lax.rem(my_head + 1 + turn * batch + b, HEADS)
            piece = attended[b * tokens : (b + 1) * tokens]
            if turn == 1 and b == batch - 1:
                att_in[my_head] = piece
            else:
                att_out[j] = piece
                remote(
                    att_out.at[j], att_in.at[my_head], att_send.at[j], att_recv.at[my_head],
                    j * reps + my_rep,
                ).start()

    @pl.loop(1, HEADS)
    def _(step):
        head = lax.rem(my_head + step, HEADS)
        remote(
            heads_out.at[head], heads_in.at[me], head_send.at[head], head_recv.at[me],
            head * reps + my_rep,
        ).wait_send()

    @pl.loop(1, reps)
    def _(step):
        @pl.loop(0, HEADS)
        def _(turn):
            share(step, lax.rem(my_head + turn, HEADS) * reps + my_rep).wait_send()

    @pl.loop(1, HEADS)
    def _(step):
        other = lax.rem(my_head + HEADS - step, HEADS)
        remote(
            att_out.at[other], att_in.at[other], att_send.at[other], att_recv.at[other],
            other * reps + my_rep,
        ).wait()

    result = jnp.zeros((tokens, width), jnp.float32)
    for h in range(0, HEADS, 2):
        both = jnp.concatenate([att_in[h], att_in[h + 1]], axis=1)
        result = result + jnp.dot(
            both,
            wo_pad[h : h + 2].reshape(2 * LANES, width),
            preferred_element_type=jnp.float32,
        )
    out_ref[...] = result.astype(jnp.bfloat16)


def on_device(tokens, owner, slot_map, sizes, w_query, w_key, w_value, w_out):
    shards = lax.axis_size("ctx")
    rows, width = tokens.shape
    slots = slot_map.shape[2]
    padded = -(-slots // 16) * 16
    merged_rows = rows // 2
    model = w_query.shape[1]
    pack = 2 * LANES
    reps = shards // HEADS
    vmem = pl.BlockSpec(memory_space=pltpu.VMEM)
    hbm = pl.BlockSpec(memory_space=pl.ANY)
    bf16 = jnp.bfloat16
    dma = pltpu.SemaphoreType.DMA
    aligned = -(-rows // LANES) * LANES
    return pl.pallas_call(
        functools.partial(kernel, shards),
        out_shape=jax.ShapeDtypeStruct((rows, width), bf16),
        in_specs=[vmem] * 4 + [hbm] * 4,
        out_specs=vmem,
        scratch_shapes=[
            pltpu.VMEM((width, model), bf16),
            pltpu.VMEM((width, model), bf16),
            pltpu.VMEM((width, model), bf16),
            pltpu.VMEM((HEADS, HEAD, width), bf16),
            pltpu.VMEM((HEADS, LANES, width), bf16),
            pltpu.VMEM((shards, shards, slots), jnp.int32),
            pltpu.VMEM((shards, slots, width + LANES), bf16),
            pltpu.VMEM((shards, slots, width + LANES), bf16),
            pltpu.VMEM((shards * padded, width + LANES), bf16),
            pltpu.VMEM((8, aligned), jnp.int32),
            pltpu.VMEM((HEADS, 8, aligned), jnp.int32),
            pltpu.VMEM((HEADS, merged_rows, pack), bf16),
            pltpu.VMEM((shards, merged_rows, pack), bf16),
            pltpu.VMEM((HEADS, rows, LANES), bf16),
            pltpu.VMEM((HEADS, rows, LANES), bf16),
            dma((4,)),
            dma((shards,)),
            dma((shards,)),
            dma((shards,)),
            dma((shards,)),
            dma((HEADS,)),
            dma((HEADS,)),
            dma((HEADS,)),
            dma((shards,)),
            dma((reps * shards,)),
            dma((HEADS,)),
            dma((HEADS,)),
            dma((1,)),
        ],
        compiler_params=pltpu.CompilerParams(
            collective_id=0, has_side_effects=True, vmem_limit_bytes=60 * 1024 * 1024
        ),
        name="merged_attention",
    )(
        tokens,
        owner,
        slot_map,
        sizes.reshape(1, rows),
        w_query,
        w_key,
        w_value,
        w_out.reshape(HEADS, HEAD, width),
    )


def solution(mesh):
    in_specs = (
        P(("groups", "ctx"), None),
        P(("groups", "ctx"), None),
        P(("groups", "ctx"), None, None),
        P(("groups", "ctx")),
        P(),
        P(),
        P(),
        P(),
    )
    out_specs = P(("groups", "ctx"), None)
    return jax.shard_map(
        on_device, mesh=mesh, in_specs=in_specs, out_specs=out_specs, check_vma=False
    )
```

time: 127 us -> 55.5 us (0.44)
  blocking collectives: 91.4 us -> 0 us
  Pallas kernels: 0 us -> 45 us
  starting transfers between devices: 11 us -> 0 us
  matrix products: 9.81 us -> 0 us
  waiting for transfers between devices: 4.09 us -> 0 us
  local copies, waits for them, and re-layouts: 6.33 us -> 10.3 us
  other arithmetic: 3.01 us -> 0 us
    pallas_call x0 -> x1, Pallas kernels: none -> 45 us  [on_device(): pl.pallas_call(functools.partial(kernel, shards), out_shape=jax.ShapeDtyp...]
    all_gather x2 -> x0, blocking collectives: 41.9 us -> none  [the longest x1 21.5 us: on_device(): keys = lax.all_gather(own_keys, 'ctx', axis=0, tiled=True)]
    unnamed x1 -> x0, blocking collectives: 35.8 us -> none
    all_to_all x1 -> x0, blocking collectives: 13.7 us -> none  [on_device(): lax.all_to_all(leaving.reshape(shards, slots, -1), 'ctx', split_axis=0, c...]
    all_to_all x2 -> x0, starting transfers between devices: 11 us -> none  [the longest x1 7.41 us: on_device(): lax.all_to_all(out_weights.reshape(shards, slots), 'ctx', split_axis=0, c...]
    dot_general x10 -> x0, matrix products: 9.81 us -> none  [the longest x1 1.8 us: on_device(): jnp.dot(merged, w_query, preferred_element_type=jnp.float32)]
    unnamed x14 -> x10, local copies, waits for them, and re-layouts: 1.32 us -> 10.3 us
    all_to_all x2 -> x0, waiting for transfers between devices: 4.09 us -> none  [the longest x1 4.09 us: on_device(): lax.all_to_all(out_weights.reshape(shards, slots), 'ctx', split_axis=0, c...]
  transfers between devices with their start and end apart: 2 -> 0, of which waited for: 1 -> 0; matrix products, arithmetic and copies ran while one was open for 3% -> 0% of each run, Pallas kernels for 0% -> 0%
where the time goes in v1:
time: 55.5 us; the launch traced here: 55.3 us
  Pallas kernels  45 us (81%)
  local copies, waits for them, and re-layouts  10.3 us (19%)
    pallas_call x1, Pallas kernels, on_device(): pl.pallas_call(functools.partial(kernel, shards), out_shape=jax.ShapeDtyp...  45 us
    unnamed x10, local copies, waits for them, and re-layouts  10.3 us

profile of v1, /device:TPU:0, one launch (start us, length us, event | category | flops | bytes accessed | tf_op | source)
XLA Modules:
  0.0 55.3 jit_solution(3420689719090641940)
XLA Ops:
  0.0 1.4 %copy.10.slot_ref = s32[1,16,12]{2,1,0:T(8,128)} copy(s32[1,16,12]{1,0,2:T(1,128)} %param.10) | data formatting | bytes 1536 | tf_op args[2]
  1.4 1.4 %copy.9.owner_ref = s32[96,1]{1,0:T(8,128)} copy(s32[96,1]{0,1:T(1,128)} %param.9) | data formatting | bytes 768 | tf_op args[1]
  2.7 0.0 copy-start
  2.7 2.7 %copy.11.wq_hbm = bf16[1152,576]{1,0:T(8,128)(2,1)} copy(bf16[1152,576]{0,1:T(8,128)(2,1)} %param.12) | data formatting | bytes 2654208 | tf_op args[4]
  5.4 0.0 copy-done
  5.4 0.0 copy-start.1
  5.4 1.6 %copy.12.wk_hbm = bf16[1152,576]{1,0:T(8,128)(2,1)} copy(bf16[1152,576]{0,1:T(8,128)(2,1)S(1)} %copy-done) | data formatting | bytes 2654208 | tf_op args[5]
  7.1 0.0 copy-done.1
  7.1 1.6 %copy.13.wv_hbm = bf16[1152,576]{1,0:T(8,128)(2,1)} copy(bf16[1152,576]{0,1:T(8,128)(2,1)S(1)} %copy-done.1) | data formatting | bytes 2654208 | tf_op args[6]
  8.7 45.0 %merged_attention.1 = bf16[96,1152]{1,0:T(8,128)(2,1)} custom-call(bf16[96,1152]{1,0:T(8,128)(2,1)} %tok_ref.1, s32[96,1]{1,0:T(8,128)} %copy.9.owner_ref, s32[1,16,12]{2,1,0:T(8,128)} %copy.10.slot_ref, s32[1,96]{1,0:T(1,128)} %bitcast.3, bf16[1152,576]{1,0:T(8,128)(2,1)} %copy.11.wq_hbm, bf16[1152,576]{1,0:T(8,128)(2,1)} %copy.12.wk_hbm, ...), custom_call_target="tpu_custom_call" | custom-call | tf_op jit(solution)/shard_map/merged_attention/pallas_call | solution.py:383
  53.7 1.6 %copy.15 = bf16[96,1152]{1,0:T(8,128)(2,1)} copy(bf16[96,1152]{1,0:T(8,128)(2,1)} %merged_attention.1) | data formatting | bytes 442368
Async XLA Ops:
  2.7 2.7 %copy-start = (bf16[1152,576]{0,1:T(8,128)(2,1)S(1)}, bf16[1152,576]{0,1:T(8,128)(2,1)}, u32[]{:S(2)}) copy-start(bf16[1152,576]{0,1:T(8,128)(2,1)} %param.13) | copy-start | bytes 3981316
  5.4 1.6 %copy-start.1 = (bf16[1152,576]{0,1:T(8,128)(2,1)S(1)}, bf16[1152,576]{0,1:T(8,128)(2,1)}, u32[]{:S(2)}) copy-start(bf16[1152,576]{0,1:T(8,128)(2,1)} %param.14) | copy-start | bytes 3981316
